TPU v7x, 256 devices: a whole 4x4x8 slice. The times are simulated.
256 devices in a mesh: req: 64 (over y, z, core), mlp: 4 (over x).
Axes of the slice: x: 4, y: 4, z: 8, core: 2. Of those that a mesh axis runs over, the one named last changes fastest.
Arguments:
- queries: bfloat16 [64, 2, 16, 2, 1536], P('req', None, 'mlp'), may hold values from -64 to 64
- new_kv: bfloat16 [64, 2, 16, 2, 256], P('req', None, 'mlp'), may hold values from -9 to 9
- residual: bfloat16 [64, 2, 16, 2, 1536], P('req', None, 'mlp'), may hold values from -3 to 3
- prompt_kv: bfloat16 [64, 1024, 256], P('req'), may hold values from -9 to 9
- tail_kv: bfloat16 [64, 16, 64, 256], P('req', 'mlp'), may hold values from -9 to 9
- page_pool: bfloat16 [16384, 20, 256], P(('req', 'mlp')), may hold values from -9 to 9
- page_holder: int32 [256, 64], P(('req', 'mlp')), may hold values from 0 to 63, as said below
- serve_slot: int32 [256, 64], P(('req', 'mlp')), may hold values from 0 to 63
- prompt_len: int32 [64, 2], P('req'), may hold values from 512 to 32768
- tail_len: int32 [64, 2, 16], P('req', None, 'mlp'), may hold values from 1 to 62, 496 in all within a row
- w_out: bfloat16 [1536, 1536], P('mlp'), may hold values from -0.15625 to 0.15625
- norm_mlp: float32 [1536], replicated, may hold values from 0.25 to 1.75
- w_gate: bfloat16 [1536, 4608], P(None, 'mlp'), may hold values from -0.15625 to 0.15625
- w_up: bfloat16 [1536, 4608], P(None, 'mlp'), may hold values from -0.15625 to 0.15625
- w_down: bfloat16 [4608, 1536], P('mlp'), may hold values from -0.09375 to 0.09375
- norm_final: float32 [1536], replicated, may hold values from 0.25 to 1.75
- w_score: float32 [1536], replicated, may hold values from -0.15625 to 0.15625
Outputs:
- scores: float32 [64, 2, 16, 2], P('req', None, 'mlp')
- hidden_out: bfloat16 [64, 2, 16, 2, 1536], P('req', None, 'mlp')
- tails_out: bfloat16 [64, 2, 16, 64, 256], P('req', None, 'mlp')
Inputs may be any that keep to these rules, and one draw needn't show every extreme that they name: Each row of page_holder names every req index once.
All inputs are finite; a program needn't handle non-finite values. No bound on the sum of `tail_len` on one device may be relied on, other than what follows from the above.
Results may differ from a plain program's by a relative error of at most 0.015.
Values may be sent and summed in bfloat16 or wider, within the bound.
No kernel may reach another device: no remote copies, remote signals or barrier semaphores. Data moves between devices by JAX's collectives and lax.ppermute only.
A program may use at most 64 MiB of HBM per device.

v0:
```python
import jax
import jax.numpy as jnp
from jax import lax
from jax.sharding import PartitionSpec as P


def attend(query, fresh, window, tails, plen, tlen):
    count = query.shape[0]
    size = window.shape[-1] // 2
    q = query.reshape(count, 2, -1, size)
    scale = 1.0 / jnp.sqrt(jnp.float32(size))
    s_win = (
        jnp.einsum("sthd,kd->sthk", q, window[:, :size], preferred_element_type=jnp.float32) * scale
    )
    s_tail = (
        jnp.einsum("sthd,sjd->sthj", q, tails[..., :size], preferred_element_type=jnp.float32)
        * scale
    )
    s_new = (
        jnp.einsum("sthd,sud->sthu", q, fresh[..., :size], preferred_element_type=jnp.float32)
        * scale
    )
    tpos = tlen[:, None] + jnp.arange(2, dtype=jnp.int32)[None, :]
    kw = jnp.arange(window.shape[0], dtype=jnp.int32)[None, None, None, :]
    ok_win = (kw >= window.shape[0] - plen) & (kw > tpos[:, :, None, None])
    kt = jnp.arange(tails.shape[1], dtype=jnp.int32)[None, None, None, :]
    ok_tail = kt < tlen[:, None, None, None]
    steps = jnp.arange(2, dtype=jnp.int32)
    ok_new = steps[None, None, None, :] <= steps[None, :, None, None]
    s_win = jnp.where(ok_win, s_win, -1e30)
    s_tail = jnp.where(ok_tail, s_tail, -1e30)
    s_new = jnp.where(ok_new, s_new, -1e30)
    top = jnp.maximum(jnp.maximum(s_win.max(-1), s_tail.max(-1)), s_new.max(-1))[..., None]
    e_win = jnp.where(ok_win, jnp.exp(s_win - top), 0.0)
    e_tail = jnp.where(ok_tail, jnp.exp(s_tail - top), 0.0)
    e_new = jnp.where(ok_new, jnp.exp(s_new - top), 0.0)
    total = (
        e_win.sum(-1, keepdims=True) + e_tail.sum(-1, keepdims=True) + e_new.sum(-1, keepdims=True)
    )
    p_win = (e_win / total).astype(jnp.bfloat16)
    p_tail = (e_tail / total).astype(jnp.bfloat16)
    p_new = (e_new / total).astype(jnp.bfloat16)
    out = jnp.einsum("sthk,kd->sthd", p_win, window[:, size:], preferred_element_type=jnp.float32)
    out = out + jnp.einsum(
        "sthj,sjd->sthd", p_tail, tails[..., size:], preferred_element_type=jnp.float32
    )
    out = out + jnp.einsum(
        "sthu,sud->sthd", p_new, fresh[..., size:], preferred_element_type=jnp.float32
    )
    return out.reshape(count, 2, -1).astype(jnp.bfloat16)


def extend(tails, fresh, tlen):
    rows = jnp.arange(tails.shape[1], dtype=jnp.int32)[None, :, None]
    lead = tlen[:, None, None]
    out = jnp.where(rows == lead, fresh[:, 0][:, None, :], tails)
    return jnp.where(rows == lead + 1, fresh[:, 1][:, None, :], out)


def rms_scale(values):
    return values * lax.rsqrt(jnp.mean(values * values, axis=-1, keepdims=True) + 1e-06)


def on_device(
    queries,
    new_kv,
    residual,
    prompt_kv,
    tail_kv,
    page_pool,
    page_holder,
    serve_slot,
    prompt_len,
    tail_len,
    w_out,
    norm_mlp,
    w_gate,
    w_up,
    w_down,
    norm_final,
    w_score,
):
    samp_dev = queries.shape[2]
    width = residual.shape[-1]
    kv_width = new_kv.shape[-1]
    win_rows = prompt_kv.shape[1]
    tail_rows = tail_kv.shape[2]
    outgoing = jnp.take(page_pool, serve_slot[0], axis=0)
    arrived = lax.all_to_all(outgoing, "req", split_axis=0, concat_axis=0, tiled=True)
    fetched = jnp.take(arrived, page_holder[0], axis=0).reshape(-1, kv_width)
    moved_window = fetched[:win_rows]
    moved_tails = fetched[win_rows:].reshape(samp_dev, tail_rows, kv_width)
    first = attend(
        queries[0, 0], new_kv[0, 0], prompt_kv[0], tail_kv[0], prompt_len[0, 0], tail_len[0, 0]
    )
    second = attend(
        queries[0, 1], new_kv[0, 1], moved_window, moved_tails, prompt_len[0, 1], tail_len[0, 1]
    )
    attn = jnp.stack([first, second])[None]
    tails_out = jnp.stack(
        [
            extend(tail_kv[0], new_kv[0, 0], tail_len[0, 0]),
            extend(moved_tails, new_kv[0, 1], tail_len[0, 1]),
        ]
    )[None]
    block_width = w_out.shape[0]
    position = lax.axis_index("mlp")
    every = lax.all_gather(attn, "mlp", axis=2, tiled=True)
    block = lax.dynamic_slice_in_dim(every, position * block_width, block_width, 4)
    partial_sum = jnp.dot(block.reshape(-1, block_width), w_out, preferred_element_type=jnp.float32)
    mixed = lax.psum(partial_sum, "mlp")
    res_all = lax.all_gather(residual, "mlp", axis=2, tiled=True).reshape(-1, width)
    h1_all = (res_all.astype(jnp.float32) + mixed).astype(jnp.bfloat16)
    h1_own = lax.dynamic_slice_in_dim(
        h1_all.reshape(2, -1, 2, width), position * samp_dev, samp_dev, 1
    )
    normed = (rms_scale(h1_all.astype(jnp.float32)) * norm_mlp).astype(jnp.bfloat16)
    gate = jnp.dot(normed, w_gate, preferred_element_type=jnp.float32)
    up = jnp.dot(normed, w_up, preferred_element_type=jnp.float32)
    act = (jax.nn.gelu(gate, approximate=True) * up).astype(jnp.bfloat16)
    down_terms = jnp.dot(act, w_down, preferred_element_type=jnp.float32).reshape(2, -1, 2, width)
    down_own = lax.psum_scatter(
        down_terms.astype(jnp.bfloat16), "mlp", scatter_dimension=1, tiled=True
    ).astype(jnp.float32)
    h2 = h1_own.astype(jnp.float32) + down_own
    scores = jnp.sum(rms_scale(h2) * norm_final * w_score, axis=-1)
    return (scores[None], h2.astype(jnp.bfloat16)[None], tails_out)


def solution(mesh):
    placed = (
        P("req", None, "mlp", None, None),
        P("req", None, "mlp", None, None),
        P("req", None, "mlp", None, None),
        P("req", None, None),
        P("req", "mlp", None, None),
        P(("req", "mlp"), None, None),
        P(("req", "mlp"), None),
        P(("req", "mlp"), None),
        P("req", None),
        P("req", None, "mlp"),
        P("mlp", None),
        P(),
        P(None, "mlp"),
        P(None, "mlp"),
        P("mlp", None),
        P(),
        P(),
    )
    return jax.shard_map(
        on_device,
        mesh=mesh,
        in_specs=placed,
        out_specs=(
            P("req", None, "mlp", None),
            P("req", None, "mlp", None, None),
            P("req", None, "mlp", None, None),
        ),
        check_vma=False,
    )
```

profile of v0, /device:TPU:8, one launch (start us, length us, event | category | flops | bytes accessed | tf_op | source)
XLA Modules:
  0.0 237.5 jit_solution(120826959070692707)
XLA Ops:
  9.3 3.8 %gather_fusion = bf16[64,20,256]{2,0,1:T(8,128)(2,1)} fusion(bf16[64,20,256]{2,0,1:T(8,128)(2,1)} %param.24, s32[1024]{0:T(1024)S(1)} %pad_clamp_fusion.1), kind=kCustom, calls=%fused_computation.clone | custom fusion | bytes 1310976 | tf_op jit(solution)/shard_map/jit(_take)/gather | solution.py:88
  15.7 12.3 %all-to-all-start = ((bf16[64,20,256]{2,1,0:T(8,128)(2,1)}), bf16[64,20,256]{2,1,0:T(8,128)(2,1)}, u32[]{:S(2)}, u32[]{:S(2)}) async-start(bf16[64,20,256]{2,1,0:T(8,128)(2,1)} %copy.22), calls=%async_computation | async-start | bytes 1572864 | tf_op jit(solution)/shard_map/all_to_all | solution.py:89
  36.9 1.6 fusion.66
  40.4 2.0 fusion.67
  43.8 14.0 %all_gather.6 = bf16[1,2,16,2,1536]{4,3,2,1,0:T(2,128)(2,1)} all-gather(bf16[1,2,4,2,1536]{4,3,2,1,0:T(2,128)(2,1)} %param.21), channel_id=1, replica_groups=mesh['req'=64,'mlp'=4] {'mlp'}, dimensions={2}, use_global_device_ids=true | all-gather | bytes 245760 | tf_op jit(solution)/shard_map/all_gather | solution.py:112
  59.2 1.7 reshape.390
  67.9 1.9 fusion.11
  74.3 2.1 fusion.69
  76.4 2.8 %gather_fusion.1 = bf16[64,20,256]{2,1,0:T(8,128)(2,1)} fusion(bf16[64,20,256]{2,1,0:T(8,128)(2,1)} %all-to-all-done, s32[1024]{0:T(1024)} %pad_clamp_fusion), kind=kCustom, calls=%fused_computation.1.clone | custom fusion | bytes 1310976 | tf_op jit(solution)/shard_map/jit(_take)/gather | solution.py:90
  79.2 2.2 broadcast_select_fusion
  81.4 2.0 reshape.385
  84.4 2.1 fusion.70
  86.5 1.5 fusion.71
  101.0 1.6 fusion.8
  104.8 12.1 %all-gather = bf16[2,16,2,1536]{3,2,1,0:T(2,128)(2,1)S(1)} all-gather(bf16[2,4,2,1536]{3,2,1,0:T(2,128)(2,1)S(1)} %pad_maximum_fusion), channel_id=2, replica_groups=mesh['req'=64,'mlp'=4] {'mlp'}, dimensions={1}, use_global_device_ids=true | all-gather | bytes 245760 | tf_op jit(solution)/shard_map/all_gather | solution.py:108
  119.0 2.4 %fusion.72 = f32[64,1536]{1,0:T(8,128)} fusion(bf16[64,384]{1,0:T(8,128)(2,1)} %reshape.387, bf16[384,1536]{1,0:T(8,128)(2,1)} %param.29), kind=kOutput, calls=%fused_computation.155 | convolution fusion | flops 75497472 | bytes 1622016 | tf_op jit(solution)/shard_map/dot_general | solution.py:110
  122.7 1.7 select_select_fusion.1
  124.4 44.4 %all-reduce.4.cloned.1.call-done = f32[64,1536]{1,0:T(8,128)} async-done(((f32[64,1536]{1,0:T(8,128)}), f32[64,1536]{1,0:T(8,128)}) %all-reduce.4.cloned.1.call-update) | async-done | bytes 393232 | tf_op jit(solution)/shard_map/psum | solution.py:111
  170.7 3.5 %fusion.36 = f32[64,1152]{1,0:T(8,128)} fusion(bf16[1536,1152]{1,0:T(8,128)(2,1)} %param.31, bf16[64,1536]{1,0:T(8,128)(2,1)S(1)} %get-tuple-element.7, f32[1536]{0:T(1024)S(1)} %copy-done.14, f32[64]{0:T(128)S(1)} %add_rsqrt_fusion.1), kind=kOutput, calls=%fused_computation.77 | convolution fusion | flops 226885632 | bytes 4036864 | tf_op jit(solution)/shard_map/dot_general | solution.py:118
  174.2 4.2 %convolution_convert_fusion = bf16[64,1536]{1,0:T(8,128)(2,1)} fusion(bf16[1152,1536]{1,0:T(8,128)(2,1)S(1)} %copy-done, bf16[1536,1152]{1,0:T(8,128)(2,1)} %param.32, f32[64,1152]{1,0:T(8,128)} %fusion.36, bf16[64,1536]{1,0:T(8,128)(2,1)} %copy-done.1, f32[1536]{0:T(1024)S(1)} %copy-done.14, f32[64]{0:T(128)} %copy-done.22), kind=kOutput, calls=%fused_computation.4 | convolution fusion | flops 454213632 | bytes 7772416 | tf_op jit(solution)/shard_map/dot_general | solution.py:121
  178.4 1.7 convert_element_type.95
  181.2 1.6 maximum_bitcast_fusion
  182.9 1.7 reshape.388
  184.5 42.9 %all-reduce.6.cloned.1.call-done = bf16[2,16,2,1536]{3,2,1,0:T(2,128)(2,1)} async-done(((bf16[2,16,2,1536]{3,2,1,0:T(2,128)(2,1)}), bf16[2,16,2,1536]{3,2,1,0:T(2,128)(2,1)}) %all-reduce.6.cloned.1.call-update) | async-done | bytes 196624
  (112 shorter events, 53.5 us)
Async XLA Ops:
  7.2 167.0 %copy-start = (bf16[1152,1536]{1,0:T(8,128)(2,1)S(1)}, bf16[1152,1536]{1,0:T(8,128)(2,1)}, u32[]{:S(2)}) copy-start(bf16[1152,1536]{1,0:T(8,128)(2,1)} %param.33) | copy-start | bytes 10616836
  13.1 15.4 %copy-start.21 = (s32[1,2,4]{2,1,0:T(2,128)S(1)}, s32[1,2,4]{2,1,0:T(2,128)}, u32[]{:S(2)}) copy-start(s32[1,2,4]{2,1,0:T(2,128)} %param.28) | copy-start | bytes 100
  13.1 19.4 %copy-start.23 = (s32[1,2]{1,0:T(1,128)S(1)}, s32[1,2]{1,0:T(1,128)}, u32[]{:S(2)}) copy-start(s32[1,2]{1,0:T(1,128)} %param.27) | copy-start | bytes 28
  13.1 21.2 %copy-start.17 = (bf16[1,2,4,2,256]{4,3,2,1,0:T(2,128)(2,1)S(1)}, bf16[1,2,4,2,256]{4,3,2,1,0:T(2,128)(2,1)}, u32[]{:S(2)}) copy-start(bf16[1,2,4,2,256]{4,3,2,1,0:T(2,128)(2,1)} %param.20) | copy-start | bytes 24580
  15.7 60.7 %all-to-all-start = ((bf16[64,20,256]{2,1,0:T(8,128)(2,1)}), bf16[64,20,256]{2,1,0:T(8,128)(2,1)}, u32[]{:S(2)}, u32[]{:S(2)}) async-start(bf16[64,20,256]{2,1,0:T(8,128)(2,1)} %copy.22), calls=%async_computation | async-start | bytes 1572864 | tf_op jit(solution)/shard_map/all_to_all | solution.py:89
  28.0 140.8 %all-reduce.4.cloned.1.call-start = ((), (), s32[]{:S(2)}) async-start(), calls=%async_computation.1 | async-start | bytes 786432 | tf_op jit(solution)/shard_map/psum | solution.py:111
  28.5 5.8 %copy-start.20 = (s32[4]{0:T(128)}, s32[4]{0:T(128)S(1)}, u32[]{:S(2)}) copy-start(s32[4]{0:T(128)S(1)} %get-tuple-element.21) | copy-start | bytes 52
  34.3 4.2 %copy-start.10 = (bf16[4,2,256]{2,1,0:T(2,128)(2,1)}, bf16[4,2,256]{2,1,0:T(2,128)(2,1)S(1)}, u32[]{:S(2)}) copy-start(bf16[4,2,256]{2,1,0:T(2,128)(2,1)S(1)} %get-tuple-element.12) | copy-start | bytes 12292
  34.3 4.1 %copy-start.12 = (bf16[4,2,256]{2,1,0:T(2,128)(2,1)}, bf16[4,2,256]{2,1,0:T(2,128)(2,1)S(1)}, u32[]{:S(2)}) copy-start(bf16[4,2,256]{2,1,0:T(2,128)(2,1)S(1)} %get-tuple-element.13) | copy-start | bytes 12292
  39.6 2.9 %copy-start.4 = (f32[4,2,12,64]{3,2,1,0:T(8,128)}, f32[4,2,12,64]{3,2,1,0:T(8,128)S(1)}, u32[]{:S(2)}) copy-start(f32[4,2,12,64]{3,2,1,0:T(8,128)S(1)} %get-tuple-element.33) | copy-start | bytes 73732
  83.4 9.4 %copy-start.3 = (bf16[1,4,64,256]{3,2,1,0:T(8,128)(2,1)S(1)}, bf16[1,4,64,256]{3,2,1,0:T(8,128)(2,1)}, u32[]{:S(2)}) copy-start(bf16[1,4,64,256]{3,2,1,0:T(8,128)(2,1)} %param.23) | copy-start | bytes 393220
  83.4 9.4 %copy-start.5 = (f32[4,2,12,64]{3,2,1,0:T(8,128)S(1)}, f32[4,2,12,64]{3,2,1,0:T(8,128)}, u32[]{:S(2)}) copy-start(f32[4,2,12,64]{3,2,1,0:T(8,128)} %copy-done.4) | copy-start | bytes 73732
  83.4 9.5 %copy-start.7 = (f32[1,8,12]{2,1,0:T(8,128)S(1)}, f32[1,8,12]{2,1,0:T(8,128)}, u32[]{:S(2)}) copy-start(f32[1,8,12]{2,1,0:T(8,128)} %copy-done.6) | copy-start | bytes 1156
  83.4 9.5 %copy-start.19 = (pred[4,64]{1,0:T(4,128)(4,1)S(1)}, pred[4,64]{1,0:T(4,128)(4,1)}, u32[]{:S(2)}) copy-start(pred[4,64]{1,0:T(4,128)(4,1)} %get-tuple-element.40) | copy-start | bytes 772
  83.4 9.7 %copy-start.13 = (bf16[4,2,256]{2,1,0:T(2,128)(2,1)S(1)}, bf16[4,2,256]{2,1,0:T(2,128)(2,1)}, u32[]{:S(2)}) copy-start(bf16[4,2,256]{2,1,0:T(2,128)(2,1)} %copy-done.12) | copy-start | bytes 12292
  83.4 9.7 %copy-start.18 = (f32[4,2,12,2]{2,3,1,0:T(2,128)S(1)}, f32[4,2,12,2]{2,3,1,0:T(2,128)}, u32[]{:S(2)}) copy-start(f32[4,2,12,2]{2,3,1,0:T(2,128)} %get-tuple-element.29) | copy-start | bytes 2308
  83.4 9.7 %copy-start.24 = (pred[2,2]{1,0:T(4,128)(4,1)S(1)}, pred[2,2]{1,0:T(4,128)(4,1)}, u32[]{:S(2)}) copy-start(pred[2,2]{1,0:T(4,128)(4,1)} %iota_compare_fusion.8) | copy-start | bytes 16
  84.4 2.1 copy-start.2
  92.8 7.0 %copy-start.9 = (f32[1,8,12]{2,1,0:T(8,128)S(1)}, f32[1,8,12]{2,1,0:T(8,128)}, u32[]{:S(2)}) copy-start(f32[1,8,12]{2,1,0:T(8,128)} %copy-done.8) | copy-start | bytes 1156
  92.9 8.1 %copy-start.11 = (bf16[4,2,256]{2,1,0:T(2,128)(2,1)S(1)}, bf16[4,2,256]{2,1,0:T(2,128)(2,1)}, u32[]{:S(2)}) copy-start(bf16[4,2,256]{2,1,0:T(2,128)(2,1)} %copy-done.10) | copy-start | bytes 12292
  98.4 72.3 %copy-start.14 = (f32[1536]{0:T(1024)S(1)}, f32[1536]{0:T(1024)}, u32[]{:S(2)}) copy-start(f32[1536]{0:T(1024)} %param.30) | copy-start | bytes 18436
  121.4 106.0 %all-reduce.6.cloned.1.call-start = ((), (), s32[]{:S(2)}) async-start(), calls=%async_computation.2 | async-start | bytes 393216
  174.2 5.9 %copy-start.15 = (bf16[4,1,256]{2,0,1:T(4,128)(2,1)S(1)}, bf16[4,1,256]{2,0,1:T(4,128)(2,1)}, u32[]{:S(2)}) copy-start(bf16[4,1,256]{2,0,1:T(4,128)(2,1)} %copy.46) | copy-start | bytes 6148
  174.2 6.0 %copy-start.16 = (bf16[4,1,256]{2,0,1:T(4,128)(2,1)S(1)}, bf16[4,1,256]{2,0,1:T(4,128)(2,1)}, u32[]{:S(2)}) copy-start(bf16[4,1,256]{2,0,1:T(4,128)(2,1)} %copy.47) | copy-start | bytes 6148
  (4 other events, 3.3 us)
Sparse Core Ops, SparseCore 0:
  121.5 47.1 all-reduce.3
  180.3 47.1 all-reduce.5
where the time goes:
time: 240 us; the launch traced here: 237 us
  waiting for transfers between devices  87.3 us (36%)
  local copies, waits for them, and re-layouts  34.4 us (14%)
  other arithmetic  33.8 us (14%)
  matrix products  27.1 us (11%)
  blocking collectives  26.2 us (11%)
  between operations  16.2 us (7%)
  starting transfers between devices  12.4 us (5%)
    psum x1, waiting for transfers between devices, on_device(): mixed = lax.psum(partial_sum, 'mlp')  44.4 us
    unnamed x3, waiting for transfers between devices  42.9 us
    all_gather x1, blocking collectives, on_device(): lax.all_gather(residual, 'mlp', axis=2, tiled=True).reshape(-1, width)  14 us
    all_to_all x1, starting transfers between devices, on_device(): lax.all_to_all(outgoing, 'req', split_axis=0, concat_axis=0, tiled=True)  12.3 us
    all_gather x1, blocking collectives, on_device(): every = lax.all_gather(attn, 'mlp', axis=2, tiled=True)  12.1 us
    unnamed x56, local copies, waits for them, and re-layouts  8.28 us
  transfers between devices with their start and end apart: 3, of which 2 were waited for; matrix products, arithmetic and copies ran while one was open for 17% of the time, Pallas kernels for 0%

commit v1 on v0

--- a/solution.py
+++ b/solution.py
@@ -108,7 +108,7 @@
     every = lax.all_gather(attn, "mlp", axis=2, tiled=True)
     block = lax.dynamic_slice_in_dim(every, position * block_width, block_width, 4)
     partial_sum = jnp.dot(block.reshape(-1, block_width), w_out, preferred_element_type=jnp.float32)
-    mixed = lax.psum(partial_sum, "mlp")
+    mixed = jnp.sum(lax.all_gather(partial_sum, "mlp"), axis=0)
     res_all = lax.all_gather(residual, "mlp", axis=2, tiled=True).reshape(-1, width)
     h1_all = (res_all.astype(jnp.float32) + mixed).astype(jnp.bfloat16)
     h1_own = lax.dynamic_slice_in_dim(

time: 240 us -> 208 us (0.87)
  waiting for transfers between devices: 87.3 us -> 49.1 us
  other arithmetic: 33.8 us -> 40.1 us
    psum x1 -> x0, waiting for transfers between devices: 44.4 us -> none  [on_device(): mixed = lax.psum(partial_sum, 'mlp')]
    all_gather x0 -> x1, waiting for transfers between devices: none -> 6.96 us  [on_device(): mixed = jnp.sum(lax.all_gather(partial_sum, 'mlp'), axis=0)]
    reduce_sum x0 -> x2, local copies, waits for them, and re-layouts: none -> 3.91 us  [on_device(): mixed = jnp.sum(lax.all_gather(partial_sum, 'mlp'), axis=0)]
    unnamed x56 -> x52, local copies, waits for them, and re-layouts: 8.28 us -> 4.43 us
    reduce_sum x0 -> x2, other arithmetic: none -> 3.34 us  [the longest x1 2.3 us: on_device(): mixed = jnp.sum(lax.all_gather(partial_sum, 'mlp'), axis=0)]
    convert_element_type x0 -> x2, other arithmetic: none -> 3.02 us  [the longest x1 1.8 us: on_device(): h1_all = (res_all.astype(jnp.float32) + mixed).astype(jnp.bfloat16)]
  transfers between devices with their start and end apart: 3 -> 3, of which waited for: 2 -> 2; matrix products, arithmetic and copies ran while one was open for 17% -> 19% of each run, Pallas kernels for 0% -> 0%
where the time goes in v1:
time: 208 us; the launch traced here: 206 us
  waiting for transfers between devices  49.1 us (24%)
  other arithmetic  40.1 us (19%)
  local copies, waits for them, and re-layouts  34.2 us (16%)
  matrix products  27.6 us (13%)
  blocking collectives  26.4 us (13%)
  between operations  16.2 us (8%)
  starting transfers between devices  12.4 us (6%)
    unnamed x3, waiting for transfers between devices  42.1 us
    all_gather x1, blocking collectives, on_device(): lax.all_gather(residual, 'mlp', axis=2, tiled=True).reshape(-1, width)  13.8 us
    all_gather x1, blocking collectives, on_device(): every = lax.all_gather(attn, 'mlp', axis=2, tiled=True)  12.6 us
    all_to_all x1, starting transfers between devices, on_device(): lax.all_to_all(outgoing, 'req', split_axis=0, concat_axis=0, tiled=True)  12.3 us
    all_gather x1, waiting for transfers between devices, on_device(): mixed = jnp.sum(lax.all_gather(partial_sum, 'mlp'), axis=0)  6.96 us
    unnamed x52, local copies, waits for them, and re-layouts  4.43 us
    dot_general x1, matrix products, on_device(): jnp.dot(act, w_down, preferred_element_type=jnp.float32)  4.17 us
  transfers between devices with their start and end apart: 3, of which 2 were waited for; matrix products, arithmetic and copies ran while one was open for 19% of the time, Pallas kernels for 0%

profile of v1, /device:TPU:8, one launch (start us, length us, event | category | flops | bytes accessed | tf_op | source)
XLA Modules:
  0.0 206.1 jit_solution(3830413536377131169)
XLA Ops:
  8.8 3.8 %gather_fusion = bf16[64,20,256]{2,0,1:T(8,128)(2,1)} fusion(bf16[64,20,256]{2,0,1:T(8,128)(2,1)} %param.24, s32[1024]{0:T(1024)S(1)} %pad_clamp_fusion.1), kind=kCustom, calls=%fused_computation.clone | custom fusion | bytes 1310976 | tf_op jit(solution)/shard_map/jit(_take)/gather | solution.py:88
  15.1 12.3 %all-to-all-start = ((bf16[64,20,256]{2,1,0:T(8,128)(2,1)}), bf16[64,20,256]{2,1,0:T(8,128)(2,1)}, u32[]{:S(2)}, u32[]{:S(2)}) async-start(bf16[64,20,256]{2,1,0:T(8,128)(2,1)} %copy.22), calls=%async_computation | async-start | bytes 1572864 | tf_op jit(solution)/shard_map/all_to_all | solution.py:89
  40.6 2.0 fusion.62
  48.0 1.9 fusion.11
  53.1 2.1 %fusion.64 = (f32[4,2,12]{2,1,0:T(2,128)}, f32[4,2,12,2]{2,3,1,0:T(2,128)}) fusion(bf16[4,2,12,128]{3,2,1,0:T(8,128)(2,1)} %reshape_squeeze.7, bf16[4,2,256]{2,1,0:T(2,128)(2,1)} %get-tuple-element.10, pred[2,2]{1,0:T(4,128)(4,1)} %iota_compare_fusion.8), kind=kOutput, calls=%fused_computation.152 | convolution fusion | flops 49632 | bytes 36480 | tf_op jit(solution)/shard_map/sthd,sud->sthu/dot_general | solution.py:20
  55.2 2.8 %gather_fusion.1 = bf16[64,20,256]{2,1,0:T(8,128)(2,1)} fusion(bf16[64,20,256]{2,1,0:T(8,128)(2,1)} %all-to-all-done, s32[1024]{0:T(1024)} %pad_clamp_fusion), kind=kCustom, calls=%fused_computation.1.clone | custom fusion | bytes 1310976 | tf_op jit(solution)/shard_map/jit(_take)/gather | solution.py:90
  58.0 2.2 %broadcast_select_fusion = bf16[64,20,256]{2,1,0:T(8,128)(2,1)} fusion(bf16[64,20,256]{2,1,0:T(8,128)(2,1)} %gather_fusion.1, pred[64]{0:T(512)(128)(4,1)} %compare_and_fusion.2), kind=kLoop, calls=%fused_computation.25 | loop fusion | flops 327680 | bytes 1310784 | tf_op jit(solution)/shard_map/jit(_take)/select_n | solution.py:90
  60.2 2.0 reshape.397
  63.2 2.1 fusion.65
  83.6 12.6 %all-gather = bf16[2,16,2,1536]{3,2,1,0:T(2,128)(2,1)S(1)} all-gather(bf16[2,4,2,1536]{3,2,1,0:T(2,128)(2,1)S(1)} %pad_maximum_fusion), channel_id=2, replica_groups=mesh['req'=64,'mlp'=4] {'mlp'}, dimensions={1}, use_global_device_ids=true | all-gather | bytes 245760 | tf_op jit(solution)/shard_map/all_gather | solution.py:108
  98.3 2.4 %fusion.67 = f32[64,1536]{1,0:T(8,128)} fusion(bf16[64,384]{1,0:T(8,128)(2,1)} %reshape.399, bf16[384,1536]{1,0:T(8,128)(2,1)} %param.29), kind=kOutput, calls=%fused_computation.155 | convolution fusion | flops 75497472 | bytes 1622016 | tf_op jit(solution)/shard_map/dot_general | solution.py:110
  100.8 13.8 %all_gather.12 = bf16[1,2,16,2,1536]{4,3,2,1,0:T(2,128)(2,1)} all-gather(bf16[1,2,4,2,1536]{4,3,2,1,0:T(2,128)(2,1)} %param.21), channel_id=1, replica_groups=mesh['req'=64,'mlp'=4] {'mlp'}, dimensions={2}, use_global_device_ids=true | all-gather | bytes 245760 | tf_op jit(solution)/shard_map/all_gather | solution.py:112
  114.6 1.7 reshape.402
  120.1 1.7 select_select_fusion.1
  121.8 1.8 convert_bitcast_fusion
  123.6 7.0 %all-gather.4.cloned.1.call-done = f32[256,1536]{1,0:T(8,128)} async-done(((f32[64,1536]{1,0:T(8,128)}), f32[256,1536]{1,0:T(8,128)}) %all-gather.4.cloned.1.call-update) | async-done | bytes 1572880 | tf_op jit(solution)/shard_map/all_gather | solution.py:111
  130.6 2.3 %reduce_sum.100 = f32[64,1536]{1,0:T(8,128)} reduce(f32[4,64,1536]{2,1,0:T(8,128)} %bitcast.156, f32[]{:T(128)} %constant.6.clone.1), dimensions={0}, to_apply=%region_12.14 | reduce | flops 294912 | bytes 1966084 | tf_op jit(solution)/shard_map/reduce_sum | solution.py:111
  132.9 2.0 reduce_sum.102
  138.7 3.4 %fusion.68 = f32[64,1152]{1,0:T(8,128)} fusion(bf16[64,1536]{1,0:T(8,128)(2,1)S(1)} %multiply_convert_fusion, bf16[1536,1152]{1,0:T(8,128)(2,1)} %param.31), kind=kOutput, calls=%fused_computation.156 | convolution fusion | flops 226492416 | bytes 4030464 | tf_op jit(solution)/shard_map/dot_general | solution.py:118
  142.2 4.2 %convolution_convert_fusion = bf16[64,1536]{1,0:T(8,128)(2,1)} fusion(bf16[1152,1536]{1,0:T(8,128)(2,1)S(1)} %copy-done, bf16[64,1536]{1,0:T(8,128)(2,1)} %copy-done.1, bf16[1536,1152]{1,0:T(8,128)(2,1)} %param.32, f32[64,1152]{1,0:T(8,128)} %fusion.68), kind=kOutput, calls=%fused_computation.4 | convolution fusion | flops 453820416 | bytes 7766016 | tf_op jit(solution)/shard_map/dot_general | solution.py:121
  146.4 1.7 convert_element_type.119
  150.8 2.0 reduce_sum.101
  152.7 42.1 %all-reduce.3.cloned.1.call-done = bf16[2,16,2,1536]{3,2,1,0:T(2,128)(2,1)} async-done(((bf16[2,16,2,1536]{3,2,1,0:T(2,128)(2,1)}), bf16[2,16,2,1536]{3,2,1,0:T(2,128)(2,1)}) %all-reduce.3.cloned.1.call-update) | async-done | bytes 196624
  194.9 1.7 fusion.33
  (114 shorter events, 58.4 us)
Async XLA Ops:
  7.2 135.0 %copy-start = (bf16[1152,1536]{1,0:T(8,128)(2,1)S(1)}, bf16[1152,1536]{1,0:T(8,128)(2,1)}, u32[]{:S(2)}) copy-start(bf16[1152,1536]{1,0:T(8,128)(2,1)} %param.33) | copy-start | bytes 10616836
  12.6 15.5 %copy-start.20 = (s32[1,2,4]{2,1,0:T(2,128)S(1)}, s32[1,2,4]{2,1,0:T(2,128)}, u32[]{:S(2)}) copy-start(s32[1,2,4]{2,1,0:T(2,128)} %param.28) | copy-start | bytes 100
  12.6 20.7 %copy-start.14 = (bf16[1,2,4,2,256]{4,3,2,1,0:T(2,128)(2,1)S(1)}, bf16[1,2,4,2,256]{4,3,2,1,0:T(2,128)(2,1)}, u32[]{:S(2)}) copy-start(bf16[1,2,4,2,256]{4,3,2,1,0:T(2,128)(2,1)} %param.20) | copy-start | bytes 24580
  15.1 40.1 %all-to-all-start = ((bf16[64,20,256]{2,1,0:T(8,128)(2,1)}), bf16[64,20,256]{2,1,0:T(8,128)(2,1)}, u32[]{:S(2)}, u32[]{:S(2)}) async-start(bf16[64,20,256]{2,1,0:T(8,128)(2,1)} %copy.22), calls=%async_computation | async-start | bytes 1572864 | tf_op jit(solution)/shard_map/all_to_all | solution.py:89
  27.4 103.1 %all-gather.4.cloned.1.call-start = ((), (), s32[]{:S(2)}) async-start(), calls=%async_computation.1 | async-start | bytes 1966080 | tf_op jit(solution)/shard_map/all_gather | solution.py:111
  28.1 5.9 %copy-start.19 = (s32[4]{0:T(128)}, s32[4]{0:T(128)S(1)}, u32[]{:S(2)}) copy-start(s32[4]{0:T(128)S(1)} %get-tuple-element.19) | copy-start | bytes 52
  29.4 8.8 %copy-start.17 = (pred[4,64]{1,0:T(4,128)(4,1)}, pred[4,64]{1,0:T(4,128)(4,1)S(1)}, u32[]{:S(2)}) copy-start(pred[4,64]{1,0:T(4,128)(4,1)S(1)} %get-tuple-element.38) | copy-start | bytes 772
  33.9 4.3 %copy-start.9 = (bf16[4,2,256]{2,1,0:T(2,128)(2,1)}, bf16[4,2,256]{2,1,0:T(2,128)(2,1)S(1)}, u32[]{:S(2)}) copy-start(bf16[4,2,256]{2,1,0:T(2,128)(2,1)S(1)} %get-tuple-element.11) | copy-start | bytes 12292
  62.2 9.4 %copy-start.3 = (bf16[1,4,64,256]{3,2,1,0:T(8,128)(2,1)S(1)}, bf16[1,4,64,256]{3,2,1,0:T(8,128)(2,1)}, u32[]{:S(2)}) copy-start(bf16[1,4,64,256]{3,2,1,0:T(8,128)(2,1)} %param.23) | copy-start | bytes 393220
  62.2 9.5 %copy-start.4 = (f32[4,2,12,64]{3,2,1,0:T(8,128)S(1)}, f32[4,2,12,64]{3,2,1,0:T(8,128)}, u32[]{:S(2)}) copy-start(f32[4,2,12,64]{3,2,1,0:T(8,128)} %get-tuple-element.31) | copy-start | bytes 73732
  62.2 9.5 %copy-start.5 = (f32[1,8,12]{2,1,0:T(8,128)S(1)}, f32[1,8,12]{2,1,0:T(8,128)}, u32[]{:S(2)}) copy-start(f32[1,8,12]{2,1,0:T(8,128)} %maximum_maximum_fusion.1) | copy-start | bytes 1156
  62.2 9.5 %copy-start.18 = (pred[4,64]{1,0:T(4,128)(4,1)S(1)}, pred[4,64]{1,0:T(4,128)(4,1)}, u32[]{:S(2)}) copy-start(pred[4,64]{1,0:T(4,128)(4,1)} %copy-done.17) | copy-start | bytes 772
  62.2 9.7 %copy-start.10 = (bf16[4,2,256]{2,1,0:T(2,128)(2,1)S(1)}, bf16[4,2,256]{2,1,0:T(2,128)(2,1)}, u32[]{:S(2)}) copy-start(bf16[4,2,256]{2,1,0:T(2,128)(2,1)} %copy-done.9) | copy-start | bytes 12292
  62.2 9.7 %copy-start.15 = (f32[4,2,12,2]{2,3,1,0:T(2,128)S(1)}, f32[4,2,12,2]{2,3,1,0:T(2,128)}, u32[]{:S(2)}) copy-start(f32[4,2,12,2]{2,3,1,0:T(2,128)} %get-tuple-element.27) | copy-start | bytes 2308
  62.2 9.7 %copy-start.22 = (pred[2,2]{1,0:T(4,128)(4,1)S(1)}, pred[2,2]{1,0:T(4,128)(4,1)}, u32[]{:S(2)}) copy-start(pred[2,2]{1,0:T(4,128)(4,1)} %iota_compare_fusion.8) | copy-start | bytes 16
  63.2 2.1 %copy-start.2 = (bf16[256,256]{1,0:T(8,128)(2,1)}, bf16[256,256]{1,0:T(8,128)(2,1)S(1)}, u32[]{:S(2)}) copy-start(bf16[256,256]{1,0:T(8,128)(2,1)S(1)} %slice.118) | copy-start | bytes 393220
  71.6 7.0 %copy-start.7 = (f32[1,8,12]{2,1,0:T(8,128)S(1)}, f32[1,8,12]{2,1,0:T(8,128)}, u32[]{:S(2)}) copy-start(f32[1,8,12]{2,1,0:T(8,128)} %copy-done.6) | copy-start | bytes 1156
  71.7 8.1 %copy-start.8 = (bf16[4,2,256]{2,1,0:T(2,128)(2,1)S(1)}, bf16[4,2,256]{2,1,0:T(2,128)(2,1)}, u32[]{:S(2)}) copy-start(bf16[4,2,256]{2,1,0:T(2,128)(2,1)} %get-tuple-element.10) | copy-start | bytes 12292
  76.5 39.8 %copy-start.11 = (bf16[4,2,256]{2,1,0:T(2,128)(2,1)S(1)}, bf16[4,2,256]{2,1,0:T(2,128)(2,1)}, u32[]{:S(2)}) copy-start(bf16[4,2,256]{2,1,0:T(2,128)(2,1)} %copy-done.9) | copy-start | bytes 12292
  76.5 42.9 %copy-start.21 = (s32[1,2,4]{2,1,0:T(2,128)S(1)}, s32[1,2,4]{2,1,0:T(2,128)}, u32[]{:S(2)}) copy-start(s32[1,2,4]{2,1,0:T(2,128)} %param.28) | copy-start | bytes 100
  100.7 94.1 %all-reduce.3.cloned.1.call-start = ((), (), s32[]{:S(2)}) async-start(), calls=%async_computation.2 | async-start | bytes 393216
  142.2 5.9 %copy-start.12 = (bf16[4,1,256]{2,0,1:T(4,128)(2,1)S(1)}, bf16[4,1,256]{2,0,1:T(4,128)(2,1)}, u32[]{:S(2)}) copy-start(bf16[4,1,256]{2,0,1:T(4,128)(2,1)} %copy.46) | copy-start | bytes 6148
  142.2 5.9 %copy-start.13 = (bf16[4,1,256]{2,0,1:T(4,128)(2,1)S(1)}, bf16[4,1,256]{2,0,1:T(4,128)(2,1)}, u32[]{:S(2)}) copy-start(bf16[4,1,256]{2,0,1:T(4,128)(2,1)} %copy.47) | copy-start | bytes 6148
  142.2 55.3 %copy-start.16 = (f32[1536]{0:T(1024)S(1)}, f32[1536]{0:T(1024)}, u32[]{:S(2)}) copy-start(f32[1536]{0:T(1024)} %param.35) | copy-start | bytes 18436
  (2 other events, 1.3 us)
Sparse Core Ops, SparseCore 0:
  100.9 29.6 all-gather.3
  148.2 46.6 all-reduce.2
